TPU v7x, 1024 devices: a whole 8x8x8 slice. The times are simulated.
1024 devices in a mesh: dp: 16 (over x, core), expert: 64 (over y, z).
Axes of the slice: x: 8, y: 8, z: 8, core: 2. Of those that a mesh axis runs over, the one named last changes fastest.
Arguments:
- preactivations: bfloat16 [16384, 8, 1536], P(('dp', 'expert')), may hold values from -6 to 6
- route_weights: float32 [16384, 8], P(('dp', 'expert')), may hold values from 0.05 to 0.3
- expert_ids: int32 [16384, 8], P(('dp', 'expert')), may hold values from 0 to 63, all different within a row; in each aligned block of 16 rows (0 to 15, 16 to 31, ...) at most 4 rows name the same one
- down_proj: bfloat16 [64, 4096, 768], P('expert'), may hold values from -0.21875 to 0.21875
- output_cotangent: bfloat16 [16384, 4096], P(('dp', 'expert')), may hold values from -6 to 6
Outputs:
- mixed: bfloat16 [16384, 4096], P(('dp', 'expert'))
- route_grads: float32 [16384, 8], P(('dp', 'expert'))
- pre_grads: bfloat16 [16384, 8, 1536], P(('dp', 'expert'))
- down_grads: float32 [64, 4096, 768], P('expert', 'dp')
Inputs may be any that keep to these rules, and one draw needn't show every extreme that they name: `expert_ids`: among the 128 slots of one device's tokens, no expert is named more than 4 times, a bound that some block reaches; a token's 8 experts are distinct.
All inputs are finite; a program needn't handle non-finite values.
Results may differ from a plain program's by a relative error of at most 0.017.
Values may be sent and summed in bfloat16 or wider, within the bound.
No kernel may reach another device: no remote copies, remote signals or barrier semaphores. Data moves between devices by JAX's collectives and lax.ppermute only.
A program may use at most 64 MiB of HBM per device.

v0:
```python
import jax
import jax.numpy as jnp
from jax import lax
from jax.sharding import PartitionSpec as P


def slot_matrix(expert_ids, experts, capacity):
    slot_count = expert_ids.shape[0] * expert_ids.shape[1]
    flat_ids = expert_ids.reshape(slot_count)
    onehot = (flat_ids[:, None] == lax.iota(jnp.int32, experts)[None, :]).astype(jnp.float32)
    slot_order = lax.iota(jnp.int32, slot_count)
    earlier = (slot_order[:, None] > slot_order[None, :]).astype(jnp.float32)
    before = jnp.dot(earlier, onehot, preferred_element_type=jnp.float32)
    slot_rank = jnp.sum(before * onehot, axis=1).astype(jnp.int32)
    target = flat_ids * capacity + slot_rank
    return (lax.iota(jnp.int32, experts * capacity)[:, None] == target[None, :]).astype(
        jnp.bfloat16
    )


def on_device(preactivations, route_weights, expert_ids, down_proj, output_cotangent):
    token_count, per_token, pre_width = preactivations.shape
    hidden_units = pre_width // 2
    model_width = output_cotangent.shape[1]
    experts = lax.axis_size("expert")
    capacity = min(token_count, max(2, 2 * token_count * per_token // experts))
    slot_count = token_count * per_token
    row_count = experts * capacity
    placement = slot_matrix(expert_ids, experts, capacity)
    pre_vals = preactivations.reshape(slot_count, pre_width).astype(jnp.float32)
    gate_pre = pre_vals[:, :hidden_units]
    up_pre = pre_vals[:, hidden_units:]
    sigmoid_gate = jax.nn.sigmoid(gate_pre)
    activated = gate_pre * sigmoid_gate
    hidden = (activated * up_pre).astype(jnp.bfloat16)
    cotangent = output_cotangent.astype(jnp.float32)
    scaled = (
        (route_weights[:, :, None] * cotangent[:, None, :])
        .astype(jnp.bfloat16)
        .reshape(slot_count, model_width)
    )
    send_hidden = jnp.dot(placement, hidden, preferred_element_type=jnp.float32).astype(
        jnp.bfloat16
    )
    send_hidden = send_hidden.reshape(experts, capacity, hidden_units)
    send_cot = jnp.dot(placement, scaled, preferred_element_type=jnp.float32).astype(jnp.bfloat16)
    send_cot = send_cot.reshape(experts, capacity, model_width)
    weight = down_proj[0]
    recv_hidden = lax.all_to_all(send_hidden, "expert", split_axis=0, concat_axis=0, tiled=True)
    recv_cot = lax.all_to_all(send_cot, "expert", split_axis=0, concat_axis=0, tiled=True)
    expert_out = jnp.einsum(
        "scf,df->scd", recv_hidden, weight, preferred_element_type=jnp.float32
    ).astype(jnp.bfloat16)
    hidden_grad = jnp.einsum(
        "scd,df->scf", recv_cot, weight, preferred_element_type=jnp.float32
    ).astype(jnp.bfloat16)
    returned_out = lax.all_to_all(expert_out, "expert", split_axis=0, concat_axis=0, tiled=True)
    returned_grad = lax.all_to_all(hidden_grad, "expert", split_axis=0, concat_axis=0, tiled=True)
    returned_out, returned_grad, recv_hidden, recv_cot = (
        returned_out,
        returned_grad,
        recv_hidden,
        recv_cot,
    )
    slot_outs = jnp.dot(
        placement.T,
        returned_out.reshape(row_count, model_width),
        preferred_element_type=jnp.float32,
    )
    slot_grad = jnp.dot(
        placement.T,
        returned_grad.reshape(row_count, hidden_units),
        preferred_element_type=jnp.float32,
    )
    slot_outs = slot_outs.reshape(token_count, per_token, model_width)
    mixed = jnp.einsum("tk,tkd->td", route_weights, slot_outs).astype(jnp.bfloat16)
    route_grads = jnp.einsum("tkd,td->tk", slot_outs, cotangent)
    gate_grad = slot_grad * up_pre * (sigmoid_gate * (1.0 + gate_pre * (1.0 - sigmoid_gate)))
    up_grad = slot_grad * activated
    pre_grads = (
        jnp.concatenate([gate_grad, up_grad], axis=1)
        .astype(jnp.bfloat16)
        .reshape(token_count, per_token, pre_width)
    )
    hidden_rows = recv_hidden.reshape(row_count, hidden_units)
    cot_rows = recv_cot.reshape(row_count, model_width)
    weight_grads = lax.psum_scatter(
        lax.dot_general(
            cot_rows, hidden_rows, (((0,), (0,)), ((), ())), preferred_element_type=jnp.float32
        ).astype(jnp.bfloat16),
        "dp",
        scatter_dimension=0,
        tiled=True,
    ).astype(jnp.float32)
    return (mixed, route_grads, pre_grads, weight_grads[None])


def solution(mesh):
    in_specs = (
        P(("dp", "expert"), None, None),
        P(("dp", "expert"), None),
        P(("dp", "expert"), None),
        P("expert", None, None),
        P(("dp", "expert"), None),
    )
    out_specs = (
        P(("dp", "expert"), None),
        P(("dp", "expert"), None),
        P(("dp", "expert"), None, None),
        P("expert", "dp", None),
    )
    return jax.shard_map(
        on_device, mesh=mesh, in_specs=in_specs, out_specs=out_specs, check_vma=False
    )
```

profile of v0, /device:TPU:10, one launch (start us, length us, event | category | flops | bytes accessed | tf_op | source)
XLA Modules:
  0.0 224.4 jit_solution(7662778774139387579)
XLA Ops:
  7.2 0.8 copy.19
  7.9 0.1 reshape.75
  8.0 0.2 fusion.15
  8.2 1.1 bitcast_convert_fusion.2
  9.3 0.0 copy-start.1
  9.3 0.0 copy-start.2
  9.3 0.3 convolution_convert_fusion.1
  9.6 0.8 reshape.76
  10.5 23.4 %all-to-all-start = ((bf16[64,4,768]{2,1,0:T(4,128)(2,1)}), bf16[64,4,768]{2,1,0:T(4,128)(2,1)S(1)}, u32[]{:S(2)}, u32[]{:S(2)}) async-start(bf16[64,4,768]{2,1,0:T(4,128)(2,1)} %reshape.76), calls=%async_computation | async-start | bytes 786432 | tf_op jit(solution)/shard_map/all_to_all | solution.py:49
  33.9 0.0 reduce-scatter.2.cloned.1.call-start
  33.9 0.0 copy-done.1
  34.0 0.0 copy-done.2
  34.0 0.1 copy.22
  34.1 0.1 mul.57
  34.2 2.1 convolution_convert_fusion
  36.3 2.7 %reshape.78 = bf16[64,4,4096]{2,1,0:T(4,128)(2,1)S(1)} reshape(bf16[256,4096]{1,0:T(8,128)(2,1)} %convolution_convert_fusion) | data formatting | bytes 4194304 | tf_op jit(solution)/shard_map/reshape | solution.py:47
  39.0 11.9 %all-to-all-done = bf16[64,4,768]{2,1,0:T(4,128)(2,1)S(1)} async-done(((bf16[64,4,768]{2,1,0:T(4,128)(2,1)}), bf16[64,4,768]{2,1,0:T(4,128)(2,1)S(1)}, u32[]{:S(2)}, u32[]{:S(2)}) %all-to-all-start) | async-done | bytes 393248 | tf_op jit(solution)/shard_map/all_to_all | solution.py:49
  50.9 55.6 %all_to_all.20 = bf16[64,4,4096]{2,1,0:T(4,128)(2,1)S(1)} all-to-all(bf16[64,4,4096]{2,1,0:T(4,128)(2,1)S(1)} %reshape.78), channel_id=1, replica_groups=mesh['dp'=16,'expert'=64] {'expert'}, dimensions={0} | all-to-all | bytes 4194304 | tf_op jit(solution)/shard_map/all_to_all | solution.py:50
  106.5 0.0 copy-start
  106.5 1.4 copy-done
  107.9 6.1 %bitcast_convert_fusion = bf16[4096,768]{1,0:T(8,128)(2,1)} fusion(bf16[64,4,4096]{2,1,0:T(4,128)(2,1)S(1)} %all_to_all.20, bf16[64,4,768]{2,1,0:T(4,128)(2,1)S(1)} %all-to-all-done), kind=kOutput, calls=%fused_computation | convolution fusion | flops 1613758464 | bytes 8781824 | tf_op jit(solution)/shard_map/dot_general | solution.py:88
  114.0 0.0 reduce-scatter.2.cloned.1.call-update
  114.0 4.6 %fusion.4 = bf16[64,4,4096]{2,0,1:T(8,128)(2,1)S(1)} fusion(bf16[1,4096,768]{2,1,0:T(8,128)(2,1)} %param.8, bf16[64,4,768]{2,1,0:T(4,128)(2,1)S(1)} %all-to-all-done), kind=kOutput, calls=%fused_computation.6 | convolution fusion | flops 1611661312 | bytes 8781824 | tf_op jit(solution)/shard_map/scf,df->scd/dot_general | solution.py:51
  118.7 3.0 %copy.21 = bf16[64,4,4096]{2,1,0:T(4,128)(2,1)} copy(bf16[64,4,4096]{2,0,1:T(8,128)(2,1)S(1)} %fusion.4) | data formatting | bytes 4194304 | tf_op jit(solution)/shard_map/convert_element_type | solution.py:53
  121.6 12.9 %all-to-all-start.1 = ((bf16[64,4,4096]{2,1,0:T(4,128)(2,1)}), bf16[64,4,4096]{2,1,0:T(4,128)(2,1)S(1)}, u32[]{:S(2)}, u32[]{:S(2)}) async-start(bf16[64,4,4096]{2,1,0:T(4,128)(2,1)} %copy.21), calls=%async_computation.1 | async-start | bytes 4194304 | tf_op jit(solution)/shard_map/all_to_all | solution.py:57
  134.5 0.1 copy.27
  134.6 7.4 %fusion.10 = bf16[64,4,768]{2,0,1:T(8,128)(2,1)S(1)} fusion(bf16[1,4096,768]{2,1,0:T(8,128)(2,1)} %param.8, bf16[64,4,4096]{2,1,0:T(4,128)(2,1)} %copy-done), kind=kOutput, calls=%fused_computation.12 | convolution fusion | flops 1610809344 | bytes 8781824 | tf_op jit(solution)/shard_map/scd,df->scf/dot_general | solution.py:54
  142.0 1.1 copy.24
  143.1 42.1 %all-to-all-done.1 = bf16[64,4,4096]{2,1,0:T(4,128)(2,1)S(1)} async-done(((bf16[64,4,4096]{2,1,0:T(4,128)(2,1)}), bf16[64,4,4096]{2,1,0:T(4,128)(2,1)S(1)}, u32[]{:S(2)}, u32[]{:S(2)}) %all-to-all-start.1) | async-done | bytes 2097184 | tf_op jit(solution)/shard_map/all_to_all | solution.py:57
  185.2 13.1 %all-to-all-start.3 = ((bf16[64,4,768]{2,1,0:T(4,128)(2,1)}), bf16[64,4,768]{2,1,0:T(4,128)(2,1)S(1)}, u32[]{:S(2)}, u32[]{:S(2)}) async-start(bf16[64,4,768]{2,1,0:T(4,128)(2,1)} %copy.24), calls=%async_computation.3 | async-start | bytes 786432 | tf_op jit(solution)/shard_map/all_to_all | solution.py:58
  198.3 2.1 reshape.83
  200.4 2.1 fusion.28
  202.5 0.4 fusion.37
  202.9 0.8 copy.44
  203.7 0.8 fusion.22
  204.5 0.7 copy.30
  205.1 9.3 %all-to-all-done.3 = bf16[64,4,768]{2,1,0:T(4,128)(2,1)S(1)} async-done(((bf16[64,4,768]{2,1,0:T(4,128)(2,1)}), bf16[64,4,768]{2,1,0:T(4,128)(2,1)S(1)}, u32[]{:S(2)}, u32[]{:S(2)}) %all-to-all-start.3) | async-done | bytes 393248 | tf_op jit(solution)/shard_map/all_to_all | solution.py:58
  214.5 0.1 reshape.79
  214.6 0.3 fusion.25
  214.9 0.8 pad_maximum_fusion
  215.7 0.0 reduce-scatter.2.cloned.1.call-done
  215.7 1.9 bitcast_convert_fusion.1
  (2 shorter events, 0.0 us)
Async XLA Ops:
  9.3 24.7 %copy-start.1 = (bf16[16,4096]{1,0:T(8,128)(2,1)S(1)}, bf16[16,4096]{1,0:T(8,128)(2,1)}, u32[]{:S(2)}) copy-start(bf16[16,4096]{1,0:T(8,128)(2,1)} %param.9) | copy-start | bytes 393220
  9.3 24.7 %copy-start.2 = (f32[16,8]{0,1:T(8,128)S(1)}, f32[16,8]{0,1:T(8,128)}, u32[]{:S(2)}) copy-start(f32[16,8]{0,1:T(8,128)} %param.6) | copy-start | bytes 1540
  10.5 40.4 %all-to-all-start = ((bf16[64,4,768]{2,1,0:T(4,128)(2,1)}), bf16[64,4,768]{2,1,0:T(4,128)(2,1)S(1)}, u32[]{:S(2)}, u32[]{:S(2)}) async-start(bf16[64,4,768]{2,1,0:T(4,128)(2,1)} %reshape.76), calls=%async_computation | async-start | bytes 786432 | tf_op jit(solution)/shard_map/all_to_all | solution.py:49
  33.9 181.8 %reduce-scatter.2.cloned.1.call-start = ((), (), s32[]{:S(2)}) async-start(), calls=%async_computation.5 | async-start | bytes 6684672 | tf_op jit(solution)/shard_map/reduce_scatter | solution.py:87
  106.5 1.4 copy-start
  121.6 63.5 %all-to-all-start.1 = ((bf16[64,4,4096]{2,1,0:T(4,128)(2,1)}), bf16[64,4,4096]{2,1,0:T(4,128)(2,1)S(1)}, u32[]{:S(2)}, u32[]{:S(2)}) async-start(bf16[64,4,4096]{2,1,0:T(4,128)(2,1)} %copy.21), calls=%async_computation.1 | async-start | bytes 4194304 | tf_op jit(solution)/shard_map/all_to_all | solution.py:57
  185.2 29.3 %all-to-all-start.3 = ((bf16[64,4,768]{2,1,0:T(4,128)(2,1)}), bf16[64,4,768]{2,1,0:T(4,128)(2,1)S(1)}, u32[]{:S(2)}, u32[]{:S(2)}) async-start(bf16[64,4,768]{2,1,0:T(4,128)(2,1)} %copy.24), calls=%async_computation.3 | async-start | bytes 786432 | tf_op jit(solution)/shard_map/all_to_all | solution.py:58
Sparse Core Ops, SparseCore 0:
  114.2 68.9 reduce-scatter.1
where the time goes:
time: 225 us; the launch traced here: 224 us
  waiting for transfers between devices  63.3 us (28%)
  blocking collectives  55.6 us (25%)
  starting transfers between devices  49.4 us (22%)
  matrix products  24.3 us (11%)
  between operations  14.2 us (6%)
  local copies, waits for them, and re-layouts  13.7 us (6%)
  other arithmetic  3.8 us (2%)
    all_to_all x1, blocking collectives, on_device(): lax.all_to_all(send_cot, 'expert', split_axis=0, concat_axis=0, tiled=True)  55.6 us
    all_to_all x1, waiting for transfers between devices, on_device(): lax.all_to_all(expert_out, 'expert', split_axis=0, concat_axis=0, tiled=T...  42.1 us
    all_to_all x1, starting transfers between devices, on_device(): lax.all_to_all(send_hidden, 'expert', split_axis=0, concat_axis=0, tiled=...  23.4 us
    all_to_all x1, starting transfers between devices, on_device(): lax.all_to_all(hidden_grad, 'expert', split_axis=0, concat_axis=0, tiled=...  13.1 us
    all_to_all x1, starting transfers between devices, on_device(): lax.all_to_all(expert_out, 'expert', split_axis=0, concat_axis=0, tiled=T...  12.9 us
    all_to_all x1, waiting for transfers between devices, on_device(): lax.all_to_all(send_hidden, 'expert', split_axis=0, concat_axis=0, tiled=...  11.9 us
    all_to_all x1, waiting for transfers between devices, on_device(): lax.all_to_all(hidden_grad, 'expert', split_axis=0, concat_axis=0, tiled=...  9.31 us
    dot_general x1, matrix products, on_device(): jnp.einsum('scd,df->scf', recv_cot, weight, preferred_element_type=jnp.fl...  7.4 us
  transfers between devices with their start and end apart: 4, of which 3 were waited for; matrix products, arithmetic and copies ran while one was open for 13% of the time, Pallas kernels for 0%

commit v1 on v0

v1 whole, which is shorter than its diff:
```python
import functools

import jax
import jax.numpy as jnp
from jax import lax
from jax.experimental import pallas as pl
from jax.experimental.pallas import tpu as pltpu
from jax.sharding import Mesh, PartitionSpec as P


F32 = jnp.float32
BF16 = jnp.bfloat16
CAP = 4


def iota(shape, dim):
    return lax.broadcasted_iota(jnp.int32, shape, dim)


def mm(a, b, dims=((1,), (0,))):
    return lax.dot_general(a, b, (dims, ((), ())), preferred_element_type=F32)


def by_slot(values_t, tokens):
    return jnp.concatenate(
        [jnp.broadcast_to(values_t[:, t : t + 1], (values_t.shape[0], 128)) for t in range(tokens)],
        axis=0,
    )


def gate_terms(pre_ref, hid):
    gate = pre_ref[:, :hid].astype(F32)
    up = pre_ref[:, hid:].astype(F32)
    sig = jax.nn.sigmoid(gate)
    return gate, up, sig


def prep_kernel(pre_ref, rw_ref, ids_ref, cot_ref, out_ref, *, hid, cut):
    per, tokens = ids_ref.shape
    slots = per * tokens
    rows, _ = out_ref.shape
    ids_col = by_slot(ids_ref[...].astype(F32), tokens)
    ids_row = ids_col.T
    i, j = iota((slots, slots), 0), iota((slots, slots), 1)
    earlier = jnp.where((ids_col == ids_row) & (i < j), 1.0, 0.0)
    place = ids_row[0:1] * (2.0 * CAP) + jnp.sum(earlier, axis=0, keepdims=True)
    place = place.astype(jnp.int32)
    r = iota((rows, slots), 0)
    first = jnp.where(r == place, 1.0, 0.0).astype(BF16)
    second = jnp.where(r == place + CAP, 1.0, 0.0).astype(BF16)
    of_token = jnp.where(iota((slots, tokens), 0) // per == iota((slots, tokens), 1), 1.0, 0.0).astype(BF16)
    first_tok = mm(first, of_token).astype(BF16)
    second_tok = mm(second, of_token).astype(BF16)
    gate, up, sig = gate_terms(pre_ref, hid)
    weight = by_slot(rw_ref[...], tokens)[:, 0:1]
    hidden = (gate * sig * up * weight).astype(BF16)
    d = cot_ref.shape[1]
    out_ref[:, :hid] = (mm(first, hidden) + mm(second_tok, cot_ref[:, cut : cut + hid])).astype(BF16)
    out_ref[:, hid:] = (
        mm(first_tok, cot_ref[:, :cut]) + mm(second_tok, cot_ref[:, cut + hid : d])
    ).astype(BF16)


def expert_kernel(core_ref, x_ref, w_ref, y_ref, keep_ref, send_ref, cot, hid_rows, outs, grad, *, hid, cut, step):
    n = pl.program_id(0)
    rows, _ = x_ref.shape
    half = rows // 2
    d = cot.shape[1]

    @pl.when(n == 0)
    def _():
        m, r = iota((half, rows), 0), iota((half, rows), 1)
        spot = (m // CAP) * (2 * CAP) + m % CAP
        first = jnp.where(r == spot, 1.0, 0.0).astype(BF16)
        second = jnp.where(r == spot + CAP, 1.0, 0.0).astype(BF16)
        hid_rows[...] = mm(first, x_ref[:, :hid]).astype(BF16)
        cot[:, :cut] = mm(first, x_ref[:, hid:]).astype(BF16)
        cot[:, cut:] = mm(second, x_ref[...]).astype(BF16)
        grad[...] = jnp.zeros_like(grad)

    at = pl.multiple_of(n * step, step)
    piece = step // 2
    core = core_ref[0]
    hidden = hid_rows[...]
    weight = w_ref[...]
    grad[...] += mm(cot[:, pl.ds(at, step)], weight)
    outs[:, pl.ds(at, step)] = mm(hidden, weight, ((1,), (1,))).astype(BF16)
    mine = pl.multiple_of(at + core * piece, piece)
    other = pl.multiple_of(at + (1 - core) * piece, piece)
    send_ref[...] = mm(cot[:, pl.ds(other, piece)], hidden, ((0,), (0,))).astype(BF16)
    keep_ref[...] = mm(cot[:, pl.ds(mine, piece)], hidden, ((0,), (0,))).astype(BF16)

    @pl.when(n == pl.num_programs(0) - 1)
    def _():
        r, m = iota((rows, half), 0), iota((rows, half), 1)
        spot = (m // CAP) * (2 * CAP) + m % CAP
        first = jnp.where(r == spot, 1.0, 0.0).astype(BF16)
        second = jnp.where(r == spot + CAP, 1.0, 0.0).astype(BF16)
        y_ref[:, :hid] = (
            mm(first, grad[...].astype(BF16)) + mm(second, outs[:, cut : cut + hid])
        ).astype(BF16)
        y_ref[:, hid:] = (mm(first, outs[:, :cut]) + mm(second, outs[:, cut + hid : d])).astype(BF16)


def finish_kernel(y_ref, pre_ref, rw_ref, ids_ref, mixed_ref, route_ref, grads_ref, *, hid, cut):
    per, tokens = ids_ref.shape
    slots = per * tokens
    rows, _ = y_ref.shape
    ids_col = by_slot(ids_ref[...].astype(F32), tokens)
    ids_row = ids_col.T
    i, j = iota((slots, slots), 0), iota((slots, slots), 1)
    earlier = jnp.where((ids_col == ids_row) & (j < i), 1.0, 0.0)
    place = ids_col[:, 0:1] * (2.0 * CAP) + jnp.sum(earlier, axis=1, keepdims=True)
    place = place.astype(jnp.int32)
    r = iota((slots, rows), 1)
    first = jnp.where(r == place, 1.0, 0.0).astype(BF16)
    second = jnp.where(r == place + CAP, 1.0, 0.0).astype(BF16)
    of_token = jnp.where(iota((tokens, slots), 1) // per == iota((tokens, slots), 0), 1.0, 0.0).astype(BF16)
    first_tok = mm(of_token, first).astype(BF16)
    second_tok = mm(of_token, second).astype(BF16)
    grad = mm(first, y_ref[:, :hid])
    mixed_ref[:, :cut] = mm(first_tok, y_ref[:, hid:]).astype(BF16)
    mixed_ref[:, cut:] = mm(second_tok, y_ref[...]).astype(BF16)
    gate, up, sig = gate_terms(pre_ref, hid)
    act = gate * sig
    hidden = (act * up).astype(BF16).astype(F32)
    total = jnp.sum(grad * hidden, axis=1, keepdims=True)
    spread = jnp.broadcast_to(total, (slots, 128)).reshape(tokens, per, 128)
    lane, tok = iota((tokens, per, 128), 2), iota((tokens, per, 128), 0)
    route_ref[...] = jnp.sum(jnp.where(lane == tok, spread, 0.0), axis=0)[:, :tokens]
    scaled = grad * by_slot(rw_ref[...], tokens)[:, 0:1]
    grads_ref[:, :hid] = (scaled * up * (sig * (1.0 + gate * (1.0 - sig)))).astype(BF16)
    grads_ref[:, hid:] = (scaled * act).astype(BF16)


def on_device(preactivations, route_weights, expert_ids, down_proj, output_cotangent):
    tokens, per, pre_width = preactivations.shape
    hid = pre_width // 2
    d = output_cotangent.shape[1]
    experts = lax.axis_size(("y", "z"))
    group = lax.axis_size("x")
    rows = experts * 2 * CAP
    width = (hid + d) // 2
    cut = width - hid
    slots = tokens * per
    step = d // group
    piece = step // 2
    pre = preactivations.reshape(slots, pre_width)
    rw_t, ids_t = route_weights.T, expert_ids.T
    core = lax.axis_index("c").astype(jnp.int32).reshape(1)

    send = pl.pallas_call(
        functools.partial(prep_kernel, hid=hid, cut=cut),
        out_shape=jax.ShapeDtypeStruct((rows, width), BF16),
        name="prep",
    )(pre, rw_t, ids_t, output_cotangent)
    recv = lax.all_to_all(
        send.reshape(experts, 2 * CAP, width), ("y", "z"), split_axis=0, concat_axis=0, tiled=True
    ).reshape(rows, width)
    back, keep, give = pl.pallas_call(
        functools.partial(expert_kernel, hid=hid, cut=cut, step=step),
        out_shape=(
            jax.ShapeDtypeStruct((rows, width), BF16),
            jax.ShapeDtypeStruct((d // 2, hid), BF16),
            jax.ShapeDtypeStruct((d // 2, hid), BF16),
        ),
        grid_spec=pltpu.PrefetchScalarGridSpec(
            num_scalar_prefetch=1,
            grid=(group,),
            in_specs=[
                pl.BlockSpec((rows, width), lambda n, c: (0, 0)),
                pl.BlockSpec((step, hid), lambda n, c: (n, 0)),
            ],
            out_specs=(
                pl.BlockSpec((rows, width), lambda n, c: (0, 0)),
                pl.BlockSpec((piece, hid), lambda n, c: (n, 0)),
                pl.BlockSpec((piece, hid), lambda n, c: (n, 0)),
            ),
            scratch_shapes=[
                pltpu.VMEM((rows // 2, d), BF16),
                pltpu.VMEM((rows // 2, hid), BF16),
                pltpu.VMEM((rows // 2, d), BF16),
                pltpu.VMEM((rows // 2, hid), F32),
            ],
        ),
        name="expert",
    )(core, recv, down_proj[0])
    got = lax.ppermute(give, "c", [(0, 1), (1, 0)])
    home = lax.all_to_all(
        back.reshape(experts, 2 * CAP, width), ("y", "z"), split_axis=0, concat_axis=0, tiled=True
    ).reshape(rows, width)
    pair = (keep.astype(F32) + got.astype(F32)).astype(BF16)
    weight_grads = lax.psum_scatter(pair, "x", scatter_dimension=0, tiled=True).astype(F32)
    mixed, route_t, grads = pl.pallas_call(
        functools.partial(finish_kernel, hid=hid, cut=cut),
        out_shape=(
            jax.ShapeDtypeStruct((tokens, d), BF16),
            jax.ShapeDtypeStruct((per, tokens), F32),
            jax.ShapeDtypeStruct((slots, pre_width), BF16),
        ),
        name="finish",
    )(home, pre, rw_t, ids_t)
    return mixed, route_t.T, grads.reshape(tokens, per, pre_width), weight_grads[None]


def solution(mesh):
    fine = Mesh(mesh.devices.reshape(8, 2, 8, 8), ("x", "c", "y", "z"))
    every = ("x", "c", "y", "z")
    in_specs = (
        P(every, None, None),
        P(every, None),
        P(every, None),
        P(("y", "z"), None, None),
        P(every, None),
    )
    out_specs = (
        P(every, None),
        P(every, None),
        P(every, None, None),
        P(("y", "z"), ("x", "c"), None),
    )
    return jax.shard_map(
        on_device, mesh=fine, in_specs=in_specs, out_specs=out_specs, check_vma=False
    )
```

time: 225 us -> 217 us (0.964)
  the two profiles are of different devices: /device:TPU:10 before, /device:TPU:58 now
where the time goes in v1:
time: 217 us
  blocking collectives  73.8 us (34%)
  waiting for transfers between devices  70.8 us (33%)
  starting transfers between devices  24.8 us (11%)
  Pallas kernels  23.4 us (11%)
  between operations  14.1 us (6%)
  other arithmetic  6.43 us (3%)
  local copies, waits for them, and re-layouts  3.18 us (1%)
    all_to_all x1, blocking collectives, on_device(): lax.all_to_all(back.reshape(experts, 2 * CAP, width), ('y', 'z'), split_a...  73.8 us
    all_to_all x1, waiting for transfers between devices, on_device(): lax.all_to_all(send.reshape(experts, 2 * CAP, width), ('y', 'z'), split_a...  65 us
    all_to_all x1, starting transfers between devices, on_device(): lax.all_to_all(send.reshape(experts, 2 * CAP, width), ('y', 'z'), split_a...  22.9 us
    pallas_call x1, Pallas kernels, on_device(): pl.pallas_call(functools.partial(expert_kernel, hid=hid, cut=cut, step=st...  15.3 us
    ppermute x1, waiting for transfers between devices, on_device(): got = lax.ppermute(give, 'c', [(0, 1), (1, 0)])  5.84 us
    convert_element_type x1, other arithmetic, on_device(): pair = (keep.astype(F32) + got.astype(F32)).astype(BF16)  4.5 us
    pallas_call x1, Pallas kernels, on_device(): pl.pallas_call(functools.partial(prep_kernel, hid=hid, cut=cut), out_shap...  4.45 us
  transfers between devices with their start and end apart: 3, of which 2 were waited for; matrix products, arithmetic and copies ran while one was open for 0% of the time, Pallas kernels for 2%

profile of v1, /device:TPU:58, one launch (start us, length us, event | category | flops | bytes accessed | tf_op | source)
XLA Modules:
  0.0 216.6 jit_solution(1455081862953527528)
XLA Ops:
  7.2 4.5 %prep.1 = bf16[512,2432]{1,0:T(8,128)(2,1)} custom-call(bf16[128,1536]{1,0:T(8,128)(2,1)} %bitcast.19, f32[8,16]{1,0:T(8,128)} %bitcast.21, s32[8,16]{1,0:T(8,128)} %bitcast.23, bf16[16,4096]{1,0:T(8,128)(2,1)} %cot_ref.1), custom_call_target="tpu_custom_call" | custom-call | tf_op jit(solution)/shard_map/prep/pallas_call | solution.py:152
  11.6 22.9 %all-to-all-start = ((bf16[64,8,2432]{2,1,0:T(8,128)(2,1)}), bf16[64,8,2432]{2,1,0:T(8,128)(2,1)S(1)}, u32[]{:S(2)}, u32[]{:S(2)}) async-start(bf16[64,8,2432]{2,1,0:T(8,128)(2,1)} %bitcast.15), calls=%async_computation | async-start | bytes 4980736 | tf_op jit(solution)/shard_map/all_to_all | solution.py:157
  34.5 0.0 reduce-scatter.2.cloned.1.call-start
  34.6 65.0 %all-to-all-done = bf16[64,8,2432]{2,1,0:T(8,128)(2,1)S(1)} async-done(((bf16[64,8,2432]{2,1,0:T(8,128)(2,1)}), bf16[64,8,2432]{2,1,0:T(8,128)(2,1)S(1)}, u32[]{:S(2)}, u32[]{:S(2)}) %all-to-all-start) | async-done | bytes 2490400 | tf_op jit(solution)/shard_map/all_to_all | solution.py:157
  99.5 0.0 copy-start
  99.5 1.5 copy-done
  101.0 15.3 %expert.1 = (bf16[512,2432]{1,0:T(8,128)(2,1)}, bf16[2048,768]{1,0:T(8,128)(2,1)}, bf16[2048,768]{1,0:T(8,128)(2,1)}) custom-call(s32[1]{0:T(128)} %bitcast.core_ref, bf16[512,2432]{1,0:T(8,128)(2,1)} %bitcast.14, bf16[4096,768]{1,0:T(8,128)(2,1)} %bitcast.17), custom_call_target="tpu_custom_call" | custom-call | tf_op jit(solution)/shard_map/expert/pallas_call | solution.py:160
  116.4 1.9 collective-permute-start
  118.3 5.8 %collective-permute-done = bf16[2048,768]{1,0:T(8,128)(2,1)S(1)} collective-permute-done((bf16[2048,768]{1,0:T(8,128)(2,1)}, bf16[2048,768]{1,0:T(8,128)(2,1)S(1)}, u32[]{:S(2)}, u32[]{:S(2)}) %collective-permute-start) | collective-permute-done | bytes 3145760 | tf_op jit(solution)/shard_map/ppermute | solution.py:188
  124.1 4.5 %add_convert_fusion = bf16[2048,768]{1,0:T(8,128)(2,1)} fusion(bf16[2048,768]{1,0:T(8,128)(2,1)S(1)} %collective-permute-done, bf16[2048,768]{1,0:T(8,128)(2,1)} %get-tuple-element.14), kind=kLoop, calls=%fused_computation | loop fusion | flops 6291456 | bytes 9437184 | tf_op jit(solution)/shard_map/convert_element_type | solution.py:192
  128.6 0.0 copy-start.1
  128.6 0.0 reduce-scatter.2.cloned.1.call-update
  128.6 1.7 copy-done.1
  130.3 73.8 %all_to_all.10 = bf16[64,8,2432]{2,1,0:T(8,128)(2,1)} all-to-all(bf16[64,8,2432]{2,1,0:T(8,128)(2,1)S(1)} %bitcast.18), channel_id=1, replica_groups=mesh['x'=8,'c'=2,'y'=8,'z'=8] {'y','z'}, dimensions={0} | all-to-all | bytes 4980736 | tf_op jit(solution)/shard_map/all_to_all | solution.py:189
  204.1 3.7 %finish.1 = (bf16[16,4096]{1,0:T(8,128)(2,1)}, f32[8,16]{1,0:T(8,128)}, bf16[128,1536]{1,0:T(8,128)(2,1)}) custom-call(bf16[512,2432]{1,0:T(8,128)(2,1)} %bitcast.16, bf16[128,1536]{1,0:T(8,128)(2,1)} %bitcast.20, f32[8,16]{1,0:T(8,128)} %bitcast.22, s32[8,16]{1,0:T(8,128)} %bitcast.24), custom_call_target="tpu_custom_call" | custom-call | tf_op jit(solution)/shard_map/finish/pallas_call | solution.py:194
  207.8 0.0 reduce-scatter.2.cloned.1.call-done
  207.8 1.9 bitcast_convert_fusion
Async XLA Ops:
  11.6 87.9 %all-to-all-start = ((bf16[64,8,2432]{2,1,0:T(8,128)(2,1)}), bf16[64,8,2432]{2,1,0:T(8,128)(2,1)S(1)}, u32[]{:S(2)}, u32[]{:S(2)}) async-start(bf16[64,8,2432]{2,1,0:T(8,128)(2,1)} %bitcast.15), calls=%async_computation | async-start | bytes 4980736 | tf_op jit(solution)/shard_map/all_to_all | solution.py:157
  34.5 173.3 %reduce-scatter.2.cloned.1.call-start = ((), (), s32[]{:S(2)}) async-start(), calls=%async_computation.3 | async-start | bytes 3538944 | tf_op jit(solution)/shard_map/reduce_scatter | solution.py:193
  99.5 1.5 copy-start
  116.4 7.8 %collective-permute-start = (bf16[2048,768]{1,0:T(8,128)(2,1)}, bf16[2048,768]{1,0:T(8,128)(2,1)S(1)}, u32[]{:S(2)}, u32[]{:S(2)}) collective-permute-start(bf16[2048,768]{1,0:T(8,128)(2,1)} %get-tuple-element.15), channel_id=1, source_target_pairs={{0,64},{64,0},{1,65},{65,1},{2,66},{66,2},{3,67},{67,3},{4,68},{68... | collective-permute-start | bytes 9437192 | tf_op jit(solution)/shard_map/ppermute | solution.py:188
  128.6 1.7 copy-start.1
Sparse Core Ops, SparseCore 0:
  128.8 48.1 reduce-scatter.1

commit v2 on v1

--- a/solution.py
+++ b/solution.py
@@ -35,7 +35,7 @@
     return gate, up, sig
 
 
-def prep_kernel(pre_ref, rw_ref, ids_ref, cot_ref, out_ref, *, hid, cut):
+def prep_kernel(core_ref, pre_ref, rw_ref, ids_ref, cot_ref, out_ref, *, hid, cut):
     per, tokens = ids_ref.shape
     slots = per * tokens
     rows, _ = out_ref.shape
@@ -61,7 +61,7 @@
     ).astype(BF16)
 
 
-def expert_kernel(core_ref, x_ref, w_ref, y_ref, keep_ref, send_ref, cot, hid_rows, outs, grad, *, hid, cut, step):
+def expert_kernel(core_ref, x_ref, w_ref, y_ref, mine_ref, give_ref, cot, outs, grad, *, hid, cut, step):
     n = pl.program_id(0)
     rows, _ = x_ref.shape
     half = rows // 2
@@ -73,7 +73,9 @@
         spot = (m // CAP) * (2 * CAP) + m % CAP
         first = jnp.where(r == spot, 1.0, 0.0).astype(BF16)
         second = jnp.where(r == spot + CAP, 1.0, 0.0).astype(BF16)
-        hid_rows[...] = mm(first, x_ref[:, :hid]).astype(BF16)
+        hidden = mm(first, x_ref[:, :hid]).astype(BF16)
+        mine_ref[:, :hid] = hidden
+        give_ref[:, :hid] = hidden
         cot[:, :cut] = mm(first, x_ref[:, hid:]).astype(BF16)
         cot[:, cut:] = mm(second, x_ref[...]).astype(BF16)
         grad[...] = jnp.zeros_like(grad)
@@ -81,14 +83,12 @@
     at = pl.multiple_of(n * step, step)
     piece = step // 2
     core = core_ref[0]
-    hidden = hid_rows[...]
     weight = w_ref[...]
     grad[...] += mm(cot[:, pl.ds(at, step)], weight)
-    outs[:, pl.ds(at, step)] = mm(hidden, weight, ((1,), (1,))).astype(BF16)
-    mine = pl.multiple_of(at + core * piece, piece)
-    other = pl.multiple_of(at + (1 - core) * piece, piece)
-    send_ref[...] = mm(cot[:, pl.ds(other, piece)], hidden, ((0,), (0,))).astype(BF16)
-    keep_ref[...] = mm(cot[:, pl.ds(mine, piece)], hidden, ((0,), (0,))).astype(BF16)
+    outs[:, pl.ds(at, step)] = mm(mine_ref[:, :hid], weight, ((1,), (1,))).astype(BF16)
+    to = pl.multiple_of(hid + n * piece, piece)
+    mine_ref[:, pl.ds(to, piece)] = cot[:, pl.ds(pl.multiple_of(at + core * piece, piece), piece)]
+    give_ref[:, pl.ds(to, piece)] = cot[:, pl.ds(pl.multiple_of(at + (1 - core) * piece, piece), piece)]
 
     @pl.when(n == pl.num_programs(0) - 1)
     def _():
@@ -102,7 +102,17 @@
         y_ref[:, hid:] = (mm(first, outs[:, :cut]) + mm(second, outs[:, cut + hid : d])).astype(BF16)
 
 
-def finish_kernel(y_ref, pre_ref, rw_ref, ids_ref, mixed_ref, route_ref, grads_ref, *, hid, cut):
+def weight_kernel(mine_ref, got_ref, out_ref, *, hid, piece):
+    n = pl.program_id(0)
+    to = pl.multiple_of(hid + n * piece, piece)
+    out_ref[...] = (
+        mm(mine_ref[:, pl.ds(to, piece)], mine_ref[:, :hid], ((0,), (0,)))
+        + mm(got_ref[:, pl.ds(to, piece)], got_ref[:, :hid], ((0,), (0,)))
+    ).astype(BF16)
+
+
+def finish_kernel(y_ref, pre_ref, rw_ref, ids_ref, sum_ref, mixed_ref, route_ref, grads_ref, down_ref, *, hid, cut):
+    down_ref[...] = sum_ref[...].astype(F32)
     per, tokens = ids_ref.shape
     slots = per * tokens
     rows, _ = y_ref.shape
@@ -149,36 +159,35 @@
     rw_t, ids_t = route_weights.T, expert_ids.T
     core = lax.axis_index("c").astype(jnp.int32).reshape(1)
 
+    whole = pl.BlockSpec((rows // 2, hid + d // 2), lambda n, *_: (0, 0))
+
     send = pl.pallas_call(
         functools.partial(prep_kernel, hid=hid, cut=cut),
         out_shape=jax.ShapeDtypeStruct((rows, width), BF16),
+        in_specs=[pl.BlockSpec(memory_space=pltpu.SMEM)] + [pl.BlockSpec(memory_space=pltpu.VMEM)] * 4,
         name="prep",
-    )(pre, rw_t, ids_t, output_cotangent)
+    )(core, pre, rw_t, ids_t, output_cotangent)
     recv = lax.all_to_all(
         send.reshape(experts, 2 * CAP, width), ("y", "z"), split_axis=0, concat_axis=0, tiled=True
     ).reshape(rows, width)
-    back, keep, give = pl.pallas_call(
+    recv = pltpu.with_memory_space_constraint(recv, pltpu.VMEM)
+    back, mine, give = pl.pallas_call(
         functools.partial(expert_kernel, hid=hid, cut=cut, step=step),
         out_shape=(
             jax.ShapeDtypeStruct((rows, width), BF16),
-            jax.ShapeDtypeStruct((d // 2, hid), BF16),
-            jax.ShapeDtypeStruct((d // 2, hid), BF16),
+            jax.ShapeDtypeStruct((rows // 2, hid + d // 2), BF16),
+            jax.ShapeDtypeStruct((rows // 2, hid + d // 2), BF16),
         ),
         grid_spec=pltpu.PrefetchScalarGridSpec(
             num_scalar_prefetch=1,
             grid=(group,),
             in_specs=[
-                pl.BlockSpec((rows, width), lambda n, c: (0, 0)),
+                pl.BlockSpec(memory_space=pltpu.VMEM),
                 pl.BlockSpec((step, hid), lambda n, c: (n, 0)),
             ],
-            out_specs=(
-                pl.BlockSpec((rows, width), lambda n, c: (0, 0)),
-                pl.BlockSpec((piece, hid), lambda n, c: (n, 0)),
-                pl.BlockSpec((piece, hid), lambda n, c: (n, 0)),
-            ),
+            out_specs=(pl.BlockSpec((rows, width), lambda n, c: (0, 0)), whole, whole),
             scratch_shapes=[
                 pltpu.VMEM((rows // 2, d), BF16),
-                pltpu.VMEM((rows // 2, hid), BF16),
                 pltpu.VMEM((rows // 2, d), BF16),
                 pltpu.VMEM((rows // 2, hid), F32),
             ],
@@ -189,18 +198,27 @@
     home = lax.all_to_all(
         back.reshape(experts, 2 * CAP, width), ("y", "z"), split_axis=0, concat_axis=0, tiled=True
     ).reshape(rows, width)
-    pair = (keep.astype(F32) + got.astype(F32)).astype(BF16)
-    weight_grads = lax.psum_scatter(pair, "x", scatter_dimension=0, tiled=True).astype(F32)
-    mixed, route_t, grads = pl.pallas_call(
+    home = pltpu.with_memory_space_constraint(home, pltpu.VMEM)
+    pair = pl.pallas_call(
+        functools.partial(weight_kernel, hid=hid, piece=piece),
+        out_shape=jax.ShapeDtypeStruct((d // 2, hid), BF16),
+        grid=(group,),
+        in_specs=[whole, whole],
+        out_specs=pl.BlockSpec((piece, hid), lambda n: (n, 0)),
+        name="weights",
+    )(mine, got)
+    weight_sum = lax.psum_scatter(pair, "x", scatter_dimension=0, tiled=True)
+    mixed, route_t, grads, down = pl.pallas_call(
         functools.partial(finish_kernel, hid=hid, cut=cut),
         out_shape=(
             jax.ShapeDtypeStruct((tokens, d), BF16),
             jax.ShapeDtypeStruct((per, tokens), F32),
             jax.ShapeDtypeStruct((slots, pre_width), BF16),
+            jax.ShapeDtypeStruct((piece, hid), F32),
         ),
         name="finish",
-    )(home, pre, rw_t, ids_t)
-    return mixed, route_t.T, grads.reshape(tokens, per, pre_width), weight_grads[None]
+    )(home, pre, rw_t, ids_t, weight_sum)
+    return mixed, route_t.T, grads.reshape(tokens, per, pre_width), down[None]
 
 
 def solution(mesh):

time: 217 us -> 209 us (0.963)
  the two profiles are of different devices: /device:TPU:58 before, /device:TPU:50 now
where the time goes in v2:
time: 209 us
  blocking collectives  161 us (77%)
  Pallas kernels  27.7 us (13%)
  between operations  14 us (7%)
  waiting for transfers between devices  3.42 us (2%)
    all_to_all x1, blocking collectives, on_device(): lax.all_to_all(send.reshape(experts, 2 * CAP, width), ('y', 'z'), split_a...  85.9 us
    all_to_all x1, blocking collectives, on_device(): lax.all_to_all(back.reshape(experts, 2 * CAP, width), ('y', 'z'), split_a...  74.7 us
    pallas_call x1, Pallas kernels, on_device(): pl.pallas_call(functools.partial(expert_kernel, hid=hid, cut=cut, step=st...  13.1 us
    pallas_call x1, Pallas kernels, on_device(): pl.pallas_call(functools.partial(weight_kernel, hid=hid, piece=piece), ou...  6.88 us
    pallas_call x1, Pallas kernels, on_device(): pl.pallas_call(functools.partial(prep_kernel, hid=hid, cut=cut), out_shap...  4.45 us
  transfers between devices with their start and end apart: 2, of which 1 were waited for; matrix products, arithmetic and copies ran while one was open for 0% of the time, Pallas kernels for 0%

profile of v2, /device:TPU:50, one launch (start us, length us, event | category | flops | bytes accessed | tf_op | source)
XLA Modules:
  0.0 208.8 jit_solution(12013075323177420262)
XLA Ops:
  7.2 0.0 reduce-scatter.2.cloned.1.call-start
  7.2 4.4 %prep.1 = bf16[512,2432]{1,0:T(8,128)(2,1)} custom-call(s32[1]{0:T(128)} %bitcast.core_ref, bf16[128,1536]{1,0:T(8,128)(2,1)} %bitcast.17, f32[8,16]{1,0:T(8,128)} %bitcast.19, s32[8,16]{1,0:T(8,128)} %bitcast.21, bf16[16,4096]{1,0:T(8,128)(2,1)} %cot_ref.1), custom_call_target="tpu_custom_call" | custom-call | tf_op jit(solution)/shard_map/prep/pallas_call | solution.py:164
  11.7 85.9 %all_to_all.10 = bf16[64,8,2432]{2,1,0:T(8,128)(2,1)S(1)} all-to-all(bf16[64,8,2432]{2,1,0:T(8,128)(2,1)} %bitcast.14), channel_id=1, replica_groups=mesh['x'=8,'c'=2,'y'=8,'z'=8] {'y','z'}, dimensions={0} | all-to-all | bytes 4980736 | tf_op jit(solution)/shard_map/all_to_all | solution.py:170
  97.6 13.1 %expert.1 = (bf16[512,2432]{1,0:T(8,128)(2,1)}, bf16[256,2816]{1,0:T(8,128)(2,1)}, bf16[256,2816]{1,0:T(8,128)(2,1)}) custom-call(s32[1]{0:T(128)} %bitcast.core_ref, bf16[512,2432]{1,0:T(8,128)(2,1)S(1)} %bitcast.13, bf16[4096,768]{1,0:T(8,128)(2,1)} %bitcast.15), custom_call_target="tpu_custom_call" | custom-call | tf_op jit(solution)/shard_map/expert/pallas_call | solution.py:174
  110.7 1.9 collective-permute-start
  112.6 3.4 %collective-permute-done.got_ref = bf16[256,2816]{1,0:T(8,128)(2,1)S(1)} collective-permute-done((bf16[256,2816]{1,0:T(8,128)(2,1)}, bf16[256,2816]{1,0:T(8,128)(2,1)S(1)}, u32[]{:S(2)}, u32[]{:S(2)}) %collective-permute-start) | collective-permute-done | bytes 1441824 | tf_op jit(solution)/shard_map/ppermute | solution.py:197
  116.0 0.0 copy-start
  116.0 1.1 copy-done
  117.2 6.9 %weights.1 = bf16[2048,768]{1,0:T(8,128)(2,1)} custom-call(bf16[256,2816]{1,0:T(8,128)(2,1)} %get-tuple-element.12.mine_ref, bf16[256,2816]{1,0:T(8,128)(2,1)} %copy-done), custom_call_target="tpu_custom_call" | custom-call | tf_op jit(solution)/shard_map/weights/pallas_call | solution.py:202
  124.1 0.0 reduce-scatter.2.cloned.1.call-update
  124.1 74.7 %all_to_all.11 = bf16[64,8,2432]{2,1,0:T(8,128)(2,1)S(1)} all-to-all(bf16[64,8,2432]{2,1,0:T(8,128)(2,1)} %bitcast.16), channel_id=1, replica_groups=mesh['x'=8,'c'=2,'y'=8,'z'=8] {'y','z'}, dimensions={0} | all-to-all | bytes 4980736 | tf_op jit(solution)/shard_map/all_to_all | solution.py:198
  198.7 0.0 reduce-scatter.2.cloned.1.call-done.sum_ref
  198.7 3.2 %finish.1 = (bf16[16,4096]{1,0:T(8,128)(2,1)}, f32[8,16]{1,0:T(8,128)}, bf16[128,1536]{1,0:T(8,128)(2,1)}, f32[256,768]{1,0:T(8,128)}) custom-call(bf16[512,2432]{1,0:T(8,128)(2,1)S(1)} %bitcast.12, bf16[128,1536]{1,0:T(8,128)(2,1)} %bitcast.18, f32[8,16]{1,0:T(8,128)} %bitcast.20, s32[8,16]{1,0:T(8,128)} %bitcast.22, ...), custom_call_target="tpu_custom_call" | custom-call | tf_op jit(solution)/shard_map/finish/pallas_call | solution.py:211
Async XLA Ops:
  7.2 191.6 %reduce-scatter.2.cloned.1.call-start = ((), (), s32[]{:S(2)}) async-start(), calls=%async_computation.3 | async-start | bytes 3538944 | tf_op jit(solution)/shard_map/reduce_scatter | solution.py:210
  110.7 5.3 %collective-permute-start = (bf16[256,2816]{1,0:T(8,128)(2,1)}, bf16[256,2816]{1,0:T(8,128)(2,1)S(1)}, u32[]{:S(2)}, u32[]{:S(2)}) collective-permute-start(bf16[256,2816]{1,0:T(8,128)(2,1)} %get-tuple-element.13), channel_id=1, source_target_pairs={{0,64},{64,0},{1,65},{65,1},{2,66},{66,2},{3,67},{67,3},{4,68},{68... | collective-permute-start | bytes 4325384 | tf_op jit(solution)/shard_map/ppermute | solution.py:197
  116.0 1.1 copy-start
Sparse Core Ops, SparseCore 0:
  124.2 48.6 reduce-scatter.1

commit v3 on v2

--- a/solution.py
+++ b/solution.py
@@ -26,6 +26,25 @@
         [jnp.broadcast_to(values_t[:, t : t + 1], (values_t.shape[0], 128)) for t in range(tokens)],
         axis=0,
     )
+
+
+def halves(block):
+    rows, w = block.shape
+    pairs = block.astype(F32).reshape(rows // 16, 2, 8, w)
+    a, b = pairs[:, 0], pairs[:, 1]
+    low = iota((rows // 16, 8, w), 1) < CAP
+    first = jnp.where(low, a, pltpu.roll(b, CAP, 1))
+    second = jnp.where(low, pltpu.roll(a, CAP, 1), b)
+    return first.reshape(rows // 2, w), second.reshape(rows // 2, w)
+
+
+def weave(first, second):
+    half, w = first.shape
+    a, b = first.reshape(half // 8, 8, w), second.reshape(half // 8, 8, w)
+    low = iota((half // 8, 8, w), 1) < CAP
+    top = jnp.where(low, a, pltpu.roll(b, CAP, 1))
+    bottom = jnp.where(low, pltpu.roll(a, CAP, 1), b)
+    return jnp.stack([top, bottom], axis=1).reshape(half * 2, w).astype(BF16)
 
 
 def gate_terms(pre_ref, hid):
@@ -55,29 +74,31 @@
     weight = by_slot(rw_ref[...], tokens)[:, 0:1]
     hidden = (gate * sig * up * weight).astype(BF16)
     d = cot_ref.shape[1]
-    out_ref[:, :hid] = (mm(first, hidden) + mm(second_tok, cot_ref[:, cut : cut + hid])).astype(BF16)
-    out_ref[:, hid:] = (
-        mm(first_tok, cot_ref[:, :cut]) + mm(second_tok, cot_ref[:, cut + hid : d])
+    out_ref[:, :hid] = mm(
+        jnp.concatenate([first, second_tok], axis=1),
+        jnp.concatenate([hidden, cot_ref[:, cut : cut + hid]], axis=0),
+    ).astype(BF16)
+    out_ref[:, hid:] = mm(
+        jnp.concatenate([first_tok, second_tok], axis=1),
+        jnp.concatenate([cot_ref[:, :cut], cot_ref[:, cut + hid : d]], axis=0),
     ).astype(BF16)
 
 
 def expert_kernel(core_ref, x_ref, w_ref, y_ref, mine_ref, give_ref, cot, outs, grad, *, hid, cut, step):
     n = pl.program_id(0)
-    rows, _ = x_ref.shape
-    half = rows // 2
-    d = cot.shape[1]
+    _, width = x_ref.shape
 
     @pl.when(n == 0)
     def _():
-        m, r = iota((half, rows), 0), iota((half, rows), 1)
-        spot = (m // CAP) * (2 * CAP) + m % CAP
-        first = jnp.where(r == spot, 1.0, 0.0).astype(BF16)
-        second = jnp.where(r == spot + CAP, 1.0, 0.0).astype(BF16)
-        hidden = mm(first, x_ref[:, :hid]).astype(BF16)
-        mine_ref[:, :hid] = hidden
-        give_ref[:, :hid] = hidden
-        cot[:, :cut] = mm(first, x_ref[:, hid:]).astype(BF16)
-        cot[:, cut:] = mm(second, x_ref[...]).astype(BF16)
+        for at in range(0, width, 128):
+            first, second = halves(x_ref[:, at : at + 128])
+            first = first.astype(BF16)
+            if at < hid:
+                mine_ref[:, at : at + 128] = first
+                give_ref[:, at : at + 128] = first
+            else:
+                cot[:, at - hid : at - hid + 128] = first
+            cot[:, cut + at : cut + at + 128] = second.astype(BF16)
         grad[...] = jnp.zeros_like(grad)
 
     at = pl.multiple_of(n * step, step)
@@ -85,21 +106,16 @@
     core = core_ref[0]
     weight = w_ref[...]
     grad[...] += mm(cot[:, pl.ds(at, step)], weight)
-    outs[:, pl.ds(at, step)] = mm(mine_ref[:, :hid], weight, ((1,), (1,))).astype(BF16)
+    outs[:, pl.ds(at, step)] = mm(mine_ref[:, :hid], weight, ((1,), (1,)))
     to = pl.multiple_of(hid + n * piece, piece)
     mine_ref[:, pl.ds(to, piece)] = cot[:, pl.ds(pl.multiple_of(at + core * piece, piece), piece)]
     give_ref[:, pl.ds(to, piece)] = cot[:, pl.ds(pl.multiple_of(at + (1 - core) * piece, piece), piece)]
 
     @pl.when(n == pl.num_programs(0) - 1)
     def _():
-        r, m = iota((rows, half), 0), iota((rows, half), 1)
-        spot = (m // CAP) * (2 * CAP) + m % CAP
-        first = jnp.where(r == spot, 1.0, 0.0).astype(BF16)
-        second = jnp.where(r == spot + CAP, 1.0, 0.0).astype(BF16)
-        y_ref[:, :hid] = (
-            mm(first, grad[...].astype(BF16)) + mm(second, outs[:, cut : cut + hid])
-        ).astype(BF16)
-        y_ref[:, hid:] = (mm(first, outs[:, :cut]) + mm(second, outs[:, cut + hid : d])).astype(BF16)
+        for at in range(0, width, 128):
+            first = grad[:, at : at + 128] if at < hid else outs[:, at - hid : at - hid + 128]
+            y_ref[:, at : at + 128] = weave(first, outs[:, cut + at : cut + at + 128])
 
 
 def weight_kernel(mine_ref, got_ref, out_ref, *, hid, piece):
@@ -128,9 +144,13 @@
     of_token = jnp.where(iota((tokens, slots), 1) // per == iota((tokens, slots), 0), 1.0, 0.0).astype(BF16)
     first_tok = mm(of_token, first).astype(BF16)
     second_tok = mm(of_token, second).astype(BF16)
-    grad = mm(first, y_ref[:, :hid])
-    mixed_ref[:, :cut] = mm(first_tok, y_ref[:, hid:]).astype(BF16)
-    mixed_ref[:, cut:] = mm(second_tok, y_ref[...]).astype(BF16)
+    both = jnp.concatenate([first_tok, second_tok], axis=0)
+    left = mm(jnp.concatenate([first, both], axis=0), y_ref[:, :hid])
+    right = mm(both, y_ref[:, hid:])
+    grad = left[:slots]
+    mixed_ref[:, :cut] = right[:tokens].astype(BF16)
+    mixed_ref[:, cut : cut + hid] = left[slots + tokens :].astype(BF16)
+    mixed_ref[:, cut + hid :] = right[tokens:].astype(BF16)
     gate, up, sig = gate_terms(pre_ref, hid)
     act = gate * sig
     hidden = (act * up).astype(BF16).astype(F32)
@@ -188,7 +208,7 @@
             out_specs=(pl.BlockSpec((rows, width), lambda n, c: (0, 0)), whole, whole),
             scratch_shapes=[
                 pltpu.VMEM((rows // 2, d), BF16),
-                pltpu.VMEM((rows // 2, d), BF16),
+                pltpu.VMEM((rows // 2, d), F32),
                 pltpu.VMEM((rows // 2, hid), F32),
             ],
         ),

time: 209 us -> 206 us (0.986)
  Pallas kernels: 27.7 us -> 25 us
where the time goes in v3:
time: 206 us
  blocking collectives  160 us (78%)
  Pallas kernels  25 us (12%)
  between operations  14 us (7%)
  waiting for transfers between devices  3.42 us (2%)
    all_to_all x1, blocking collectives, on_device(): lax.all_to_all(send.reshape(experts, 2 * CAP, width), ('y', 'z'), split_a...  85.9 us
    all_to_all x1, blocking collectives, on_device(): lax.all_to_all(back.reshape(experts, 2 * CAP, width), ('y', 'z'), split_a...  74.1 us
    pallas_call x1, Pallas kernels, on_device(): pl.pallas_call(functools.partial(expert_kernel, hid=hid, cut=cut, step=st...  11.4 us
    pallas_call x1, Pallas kernels, on_device(): pl.pallas_call(functools.partial(weight_kernel, hid=hid, piece=piece), ou...  6.88 us
  transfers between devices with their start and end apart: 2, of which 1 were waited for; matrix products, arithmetic and copies ran while one was open for 0% of the time, Pallas kernels for 0%

profile of v3, /device:TPU:50, one launch (start us, length us, event | category | flops | bytes accessed | tf_op | source)
XLA Modules:
  0.0 205.6 jit_solution(11602411691467794820)
XLA Ops:
  7.2 0.0 reduce-scatter.2.cloned.1.call-start
  7.2 3.7 %prep.1 = bf16[512,2432]{1,0:T(8,128)(2,1)} custom-call(s32[1]{0:T(128)} %bitcast.core_ref, bf16[128,1536]{1,0:T(8,128)(2,1)} %bitcast.17, f32[8,16]{1,0:T(8,128)} %bitcast.19, s32[8,16]{1,0:T(8,128)} %bitcast.21, bf16[16,4096]{1,0:T(8,128)(2,1)} %cot_ref.1), custom_call_target="tpu_custom_call" | custom-call | tf_op jit(solution)/shard_map/prep/pallas_call | solution.py:184
  10.9 85.9 %all_to_all.10 = bf16[64,8,2432]{2,1,0:T(8,128)(2,1)S(1)} all-to-all(bf16[64,8,2432]{2,1,0:T(8,128)(2,1)} %bitcast.14), channel_id=1, replica_groups=mesh['x'=8,'c'=2,'y'=8,'z'=8] {'y','z'}, dimensions={0} | all-to-all | bytes 4980736 | tf_op jit(solution)/shard_map/all_to_all | solution.py:190
  96.9 11.4 %expert.1 = (bf16[512,2432]{1,0:T(8,128)(2,1)}, bf16[256,2816]{1,0:T(8,128)(2,1)}, bf16[256,2816]{1,0:T(8,128)(2,1)}) custom-call(s32[1]{0:T(128)} %bitcast.core_ref, bf16[512,2432]{1,0:T(8,128)(2,1)S(1)} %bitcast.13, bf16[4096,768]{1,0:T(8,128)(2,1)} %bitcast.15), custom_call_target="tpu_custom_call" | custom-call | tf_op jit(solution)/shard_map/expert/pallas_call | solution.py:194
  108.2 1.9 collective-permute-start
  110.1 3.4 %collective-permute-done.got_ref = bf16[256,2816]{1,0:T(8,128)(2,1)S(1)} collective-permute-done((bf16[256,2816]{1,0:T(8,128)(2,1)}, bf16[256,2816]{1,0:T(8,128)(2,1)S(1)}, u32[]{:S(2)}, u32[]{:S(2)}) %collective-permute-start) | collective-permute-done | bytes 1441824 | tf_op jit(solution)/shard_map/ppermute | solution.py:217
  113.5 0.0 copy-start
  113.5 1.1 copy-done
  114.7 6.9 %weights.1 = bf16[2048,768]{1,0:T(8,128)(2,1)} custom-call(bf16[256,2816]{1,0:T(8,128)(2,1)} %get-tuple-element.12.mine_ref, bf16[256,2816]{1,0:T(8,128)(2,1)} %copy-done), custom_call_target="tpu_custom_call" | custom-call | tf_op jit(solution)/shard_map/weights/pallas_call | solution.py:222
  121.6 0.0 reduce-scatter.2.cloned.1.call-update
  121.6 74.1 %all_to_all.11 = bf16[64,8,2432]{2,1,0:T(8,128)(2,1)S(1)} all-to-all(bf16[64,8,2432]{2,1,0:T(8,128)(2,1)} %bitcast.16), channel_id=1, replica_groups=mesh['x'=8,'c'=2,'y'=8,'z'=8] {'y','z'}, dimensions={0} | all-to-all | bytes 4980736 | tf_op jit(solution)/shard_map/all_to_all | solution.py:218
  195.7 0.0 reduce-scatter.2.cloned.1.call-done.sum_ref
  195.7 3.1 %finish.1 = (bf16[16,4096]{1,0:T(8,128)(2,1)}, f32[8,16]{1,0:T(8,128)}, bf16[128,1536]{1,0:T(8,128)(2,1)}, f32[256,768]{1,0:T(8,128)}) custom-call(bf16[512,2432]{1,0:T(8,128)(2,1)S(1)} %bitcast.12, bf16[128,1536]{1,0:T(8,128)(2,1)} %bitcast.18, f32[8,16]{1,0:T(8,128)} %bitcast.20, s32[8,16]{1,0:T(8,128)} %bitcast.22, ...), custom_call_target="tpu_custom_call" | custom-call | tf_op jit(solution)/shard_map/finish/pallas_call | solution.py:231
Async XLA Ops:
  7.2 188.6 %reduce-scatter.2.cloned.1.call-start = ((), (), s32[]{:S(2)}) async-start(), calls=%async_computation.3 | async-start | bytes 3538944 | tf_op jit(solution)/shard_map/reduce_scatter | solution.py:230
  108.2 5.3 %collective-permute-start = (bf16[256,2816]{1,0:T(8,128)(2,1)}, bf16[256,2816]{1,0:T(8,128)(2,1)S(1)}, u32[]{:S(2)}, u32[]{:S(2)}) collective-permute-start(bf16[256,2816]{1,0:T(8,128)(2,1)} %get-tuple-element.13), channel_id=1, source_target_pairs={{0,64},{64,0},{1,65},{65,1},{2,66},{66,2},{3,67},{67,3},{4,68},{68... | collective-permute-start | bytes 4325384 | tf_op jit(solution)/shard_map/ppermute | solution.py:217
  113.5 1.1 copy-start
Sparse Core Ops, SparseCore 0:
  121.7 48.5 reduce-scatter.1

commit v4 on v3

--- a/solution.py
+++ b/solution.py
@@ -47,6 +47,13 @@
     return jnp.stack([top, bottom], axis=1).reshape(half * 2, w).astype(BF16)
 
 
+CHUNKS = (0, 1280, 1920, 2432)
+
+
+def chunk_copy(made, out_ref, sems, n, at, to):
+    return pltpu.make_async_copy(made.at[:, at:to], out_ref.at[:, at:to], sems.at[n])
+
+
 def gate_terms(pre_ref, hid):
     gate = pre_ref[:, :hid].astype(F32)
     up = pre_ref[:, hid:].astype(F32)
@@ -54,7 +61,7 @@
     return gate, up, sig
 
 
-def prep_kernel(core_ref, pre_ref, rw_ref, ids_ref, cot_ref, out_ref, *, hid, cut):
+def prep_kernel(core_ref, pre_ref, rw_ref, ids_ref, cot_ref, out_ref, made, sems, *, hid, cut):
     per, tokens = ids_ref.shape
     slots = per * tokens
     rows, _ = out_ref.shape
@@ -70,57 +77,83 @@
     of_token = jnp.where(iota((slots, tokens), 0) // per == iota((slots, tokens), 1), 1.0, 0.0).astype(BF16)
     first_tok = mm(first, of_token).astype(BF16)
     second_tok = mm(second, of_token).astype(BF16)
+    left = jnp.concatenate([first_tok, second_tok], axis=1)
+    copies = []
+    for at, to in zip((hid,) + CHUNKS[1:-1], CHUNKS[1:]):
+        made[:, at:to] = mm(
+            left, jnp.concatenate([cot_ref[:, at - hid : to - hid], cot_ref[:, cut + at : cut + to]], axis=0)
+        ).astype(BF16)
+        copies.append(chunk_copy(made, out_ref, sems, len(copies), at, to))
+        copies[-1].start()
     gate, up, sig = gate_terms(pre_ref, hid)
     weight = by_slot(rw_ref[...], tokens)[:, 0:1]
     hidden = (gate * sig * up * weight).astype(BF16)
-    d = cot_ref.shape[1]
-    out_ref[:, :hid] = mm(
+    made[:, :hid] = mm(
         jnp.concatenate([first, second_tok], axis=1),
         jnp.concatenate([hidden, cot_ref[:, cut : cut + hid]], axis=0),
     ).astype(BF16)
-    out_ref[:, hid:] = mm(
-        jnp.concatenate([first_tok, second_tok], axis=1),
-        jnp.concatenate([cot_ref[:, :cut], cot_ref[:, cut + hid : d]], axis=0),
-    ).astype(BF16)
-
-
-def expert_kernel(core_ref, x_ref, w_ref, y_ref, mine_ref, give_ref, cot, outs, grad, *, hid, cut, step):
-    n = pl.program_id(0)
+    copies.append(chunk_copy(made, out_ref, sems, len(copies), 0, hid))
+    copies[-1].start()
+    for copy in copies:
+        copy.wait()
+
+
+def expert_kernel(
+    core_ref, x_ref, w_ref, y_ref, mine_ref, give_ref, cot, outs, grad, made, kept, gift, w_buf, w_sems, y_sems, mine_sem, give_sem,
+    *, hid, cut, step,
+):
     _, width = x_ref.shape
-
-    @pl.when(n == 0)
-    def _():
-        for at in range(0, width, 128):
-            first, second = halves(x_ref[:, at : at + 128])
-            first = first.astype(BF16)
-            if at < hid:
-                mine_ref[:, at : at + 128] = first
-                give_ref[:, at : at + 128] = first
-            else:
-                cot[:, at - hid : at - hid + 128] = first
-            cot[:, cut + at : cut + at + 128] = second.astype(BF16)
-        grad[...] = jnp.zeros_like(grad)
-
-    at = pl.multiple_of(n * step, step)
+    steps = cot.shape[1] // step
     piece = step // 2
     core = core_ref[0]
-    weight = w_ref[...]
-    grad[...] += mm(cot[:, pl.ds(at, step)], weight)
-    outs[:, pl.ds(at, step)] = mm(mine_ref[:, :hid], weight, ((1,), (1,)))
-    to = pl.multiple_of(hid + n * piece, piece)
-    mine_ref[:, pl.ds(to, piece)] = cot[:, pl.ds(pl.multiple_of(at + core * piece, piece), piece)]
-    give_ref[:, pl.ds(to, piece)] = cot[:, pl.ds(pl.multiple_of(at + (1 - core) * piece, piece), piece)]
-
-    @pl.when(n == pl.num_programs(0) - 1)
-    def _():
-        for at in range(0, width, 128):
+
+    def fetch(n):
+        at = pl.multiple_of(n * step, step)
+        return pltpu.make_async_copy(w_ref.at[pl.ds(at, step)], w_buf.at[pl.ds(at, step)], w_sems.at[n])
+
+    for n in range(steps):
+        fetch(n).start()
+    for at in range(0, width, 128):
+        first, second = halves(x_ref[:, at : at + 128])
+        first = first.astype(BF16)
+        if at < hid:
+            kept[:, at : at + 128] = first
+            gift[:, at : at + 128] = first
+        else:
+            cot[:, at - hid : at - hid + 128] = first
+        cot[:, cut + at : cut + at + 128] = second.astype(BF16)
+    grad[...] = jnp.zeros_like(grad)
+
+    @pl.loop(0, steps)
+    def _(n):
+        fetch(n).wait()
+        at = pl.multiple_of(n * step, step)
+        weight = w_buf[pl.ds(at, step), :]
+        grad[...] += mm(cot[:, pl.ds(at, step)], weight)
+        outs[:, pl.ds(at, step)] = mm(kept[:, :hid], weight, ((1,), (1,)))
+        to = pl.multiple_of(hid + n * piece, piece)
+        kept[:, pl.ds(to, piece)] = cot[:, pl.ds(pl.multiple_of(at + core * piece, piece), piece)]
+        gift[:, pl.ds(to, piece)] = cot[:, pl.ds(pl.multiple_of(at + (1 - core) * piece, piece), piece)]
+
+    copies = [
+        pltpu.make_async_copy(gift, give_ref, give_sem),
+        pltpu.make_async_copy(kept, mine_ref, mine_sem),
+    ]
+    copies[0].start()
+    copies[1].start()
+    for k in range(len(CHUNKS) - 1):
+        for at in range(CHUNKS[k], CHUNKS[k + 1], 128):
             first = grad[:, at : at + 128] if at < hid else outs[:, at - hid : at - hid + 128]
-            y_ref[:, at : at + 128] = weave(first, outs[:, cut + at : cut + at + 128])
+            made[:, at : at + 128] = weave(first, outs[:, cut + at : cut + at + 128])
+        copies.append(chunk_copy(made, y_ref, y_sems, k, CHUNKS[k], CHUNKS[k + 1]))
+        copies[-1].start()
+    for copy in copies:
+        copy.wait()
 
 
 def weight_kernel(mine_ref, got_ref, out_ref, *, hid, piece):
     n = pl.program_id(0)
-    to = pl.multiple_of(hid + n * piece, piece)
+    to = pl.multiple_of(hid + n * piece, 256)
     out_ref[...] = (
         mm(mine_ref[:, pl.ds(to, piece)], mine_ref[:, :hid], ((0,), (0,)))
         + mm(got_ref[:, pl.ds(to, piece)], got_ref[:, :hid], ((0,), (0,)))
@@ -179,12 +212,15 @@
     rw_t, ids_t = route_weights.T, expert_ids.T
     core = lax.axis_index("c").astype(jnp.int32).reshape(1)
 
-    whole = pl.BlockSpec((rows // 2, hid + d // 2), lambda n, *_: (0, 0))
+    smem, vmem = pl.BlockSpec(memory_space=pltpu.SMEM), pl.BlockSpec(memory_space=pltpu.VMEM)
+    outside = pl.BlockSpec(memory_space=pl.ANY)
 
     send = pl.pallas_call(
         functools.partial(prep_kernel, hid=hid, cut=cut),
         out_shape=jax.ShapeDtypeStruct((rows, width), BF16),
-        in_specs=[pl.BlockSpec(memory_space=pltpu.SMEM)] + [pl.BlockSpec(memory_space=pltpu.VMEM)] * 4,
+        in_specs=[smem] + [vmem] * 4,
+        out_specs=pl.BlockSpec(memory_space=pl.ANY),
+        scratch_shapes=[pltpu.VMEM((rows, width), BF16), pltpu.SemaphoreType.DMA((len(CHUNKS),))],
         name="prep",
     )(core, pre, rw_t, ids_t, output_cotangent)
     recv = lax.all_to_all(
@@ -198,20 +234,21 @@
             jax.ShapeDtypeStruct((rows // 2, hid + d // 2), BF16),
             jax.ShapeDtypeStruct((rows // 2, hid + d // 2), BF16),
         ),
-        grid_spec=pltpu.PrefetchScalarGridSpec(
-            num_scalar_prefetch=1,
-            grid=(group,),
-            in_specs=[
-                pl.BlockSpec(memory_space=pltpu.VMEM),
-                pl.BlockSpec((step, hid), lambda n, c: (n, 0)),
-            ],
-            out_specs=(pl.BlockSpec((rows, width), lambda n, c: (0, 0)), whole, whole),
-            scratch_shapes=[
-                pltpu.VMEM((rows // 2, d), BF16),
-                pltpu.VMEM((rows // 2, d), F32),
-                pltpu.VMEM((rows // 2, hid), F32),
-            ],
-        ),
+        in_specs=[smem, vmem, outside],
+        out_specs=(outside, outside, outside),
+        scratch_shapes=[
+            pltpu.VMEM((rows // 2, d), BF16),
+            pltpu.VMEM((rows // 2, d), F32),
+            pltpu.VMEM((rows // 2, hid), F32),
+            pltpu.VMEM((rows, width), BF16),
+            pltpu.VMEM((rows // 2, hid + d // 2), BF16),
+            pltpu.VMEM((rows // 2, hid + d // 2), BF16),
+            pltpu.VMEM((d, hid), BF16),
+            pltpu.SemaphoreType.DMA((group,)),
+            pltpu.SemaphoreType.DMA((len(CHUNKS) - 1,)),
+            pltpu.SemaphoreType.DMA,
+            pltpu.SemaphoreType.DMA,
+        ],
         name="expert",
     )(core, recv, down_proj[0])
     got = lax.ppermute(give, "c", [(0, 1), (1, 0)])
@@ -220,11 +257,11 @@
     ).reshape(rows, width)
     home = pltpu.with_memory_space_constraint(home, pltpu.VMEM)
     pair = pl.pallas_call(
-        functools.partial(weight_kernel, hid=hid, piece=piece),
+        functools.partial(weight_kernel, hid=hid, piece=step),
         out_shape=jax.ShapeDtypeStruct((d // 2, hid), BF16),
-        grid=(group,),
-        in_specs=[whole, whole],
-        out_specs=pl.BlockSpec((piece, hid), lambda n: (n, 0)),
+        grid=(group // 2,),
+        in_specs=[pl.BlockSpec((rows // 2, hid + d // 2), lambda n: (0, 0))] * 2,
+        out_specs=pl.BlockSpec((step, hid), lambda n: (n, 0)),
         name="weights",
     )(mine, got)
     weight_sum = lax.psum_scatter(pair, "x", scatter_dimension=0, tiled=True)

time: 206 us -> 201 us (0.976)
  the two profiles are of different devices: /device:TPU:50 before, /device:TPU:48 now
where the time goes in v4:
time: 201 us
  blocking collectives  160 us (80%)
  Pallas kernels  20.2 us (10%)
  between operations  14.1 us (7%)
  waiting for transfers between devices  3.42 us (2%)
    all_to_all x1, blocking collectives, on_device(): lax.all_to_all(send.reshape(experts, 2 * CAP, width), ('y', 'z'), split_a...  86 us
    all_to_all x1, blocking collectives, on_device(): lax.all_to_all(back.reshape(experts, 2 * CAP, width), ('y', 'z'), split_a...  74.2 us
    pallas_call x1, Pallas kernels, on_device(): pl.pallas_call(functools.partial(expert_kernel, hid=hid, cut=cut, step=st...  8.36 us
    pallas_call x1, Pallas kernels, on_device(): pl.pallas_call(functools.partial(weight_kernel, hid=hid, piece=step), out...  5.42 us
  transfers between devices with their start and end apart: 2, of which 1 were waited for; matrix products, arithmetic and copies ran while one was open for 0% of the time, Pallas kernels for 0%

profile of v4, /device:TPU:48, one launch (start us, length us, event | category | flops | bytes accessed | tf_op | source)
XLA Modules:
  0.0 200.9 jit_solution(4715849291534642578)
XLA Ops:
  7.2 0.0 reduce-scatter.2.cloned.1.call-start
  7.2 3.4 %prep.1 = bf16[512,2432]{1,0:T(8,128)(2,1)} custom-call(s32[1]{0:T(128)} %bitcast.core_ref, bf16[128,1536]{1,0:T(8,128)(2,1)} %bitcast.17, f32[8,16]{1,0:T(8,128)} %bitcast.19, s32[8,16]{1,0:T(8,128)} %bitcast.21, bf16[16,4096]{1,0:T(8,128)(2,1)} %cot_ref.1), custom_call_target="tpu_custom_call" | custom-call | tf_op jit(solution)/shard_map/prep/pallas_call | solution.py:218
  10.6 86.0 %all_to_all.10 = bf16[64,8,2432]{2,1,0:T(8,128)(2,1)S(1)} all-to-all(bf16[64,8,2432]{2,1,0:T(8,128)(2,1)} %bitcast.14), channel_id=1, replica_groups=mesh['x'=8,'c'=2,'y'=8,'z'=8] {'y','z'}, dimensions={0} | all-to-all | bytes 4980736 | tf_op jit(solution)/shard_map/all_to_all | solution.py:226
  96.6 8.4 %expert.1 = (bf16[512,2432]{1,0:T(8,128)(2,1)}, bf16[256,2816]{1,0:T(8,128)(2,1)}, bf16[256,2816]{1,0:T(8,128)(2,1)}) custom-call(s32[1]{0:T(128)} %bitcast.core_ref, bf16[512,2432]{1,0:T(8,128)(2,1)S(1)} %bitcast.13, bf16[4096,768]{1,0:T(8,128)(2,1)} %bitcast.15), custom_call_target="tpu_custom_call" | custom-call | tf_op jit(solution)/shard_map/expert/pallas_call | solution.py:230
  104.9 1.9 collective-permute-start
  106.9 3.4 %collective-permute-done.got_ref = bf16[256,2816]{1,0:T(8,128)(2,1)S(1)} collective-permute-done((bf16[256,2816]{1,0:T(8,128)(2,1)}, bf16[256,2816]{1,0:T(8,128)(2,1)S(1)}, u32[]{:S(2)}, u32[]{:S(2)}) %collective-permute-start) | collective-permute-done | bytes 1441824 | tf_op jit(solution)/shard_map/ppermute | solution.py:254
  110.3 0.0 copy-start
  110.3 1.1 copy-done
  111.4 5.4 %weights.1 = bf16[2048,768]{1,0:T(8,128)(2,1)} custom-call(bf16[256,2816]{1,0:T(8,128)(2,1)} %get-tuple-element.12.mine_ref, bf16[256,2816]{1,0:T(8,128)(2,1)} %copy-done), custom_call_target="tpu_custom_call" | custom-call | tf_op jit(solution)/shard_map/weights/pallas_call | solution.py:259
  116.8 0.0 reduce-scatter.2.cloned.1.call-update
  116.8 74.2 %all_to_all.11 = bf16[64,8,2432]{2,1,0:T(8,128)(2,1)S(1)} all-to-all(bf16[64,8,2432]{2,1,0:T(8,128)(2,1)} %bitcast.16), channel_id=1, replica_groups=mesh['x'=8,'c'=2,'y'=8,'z'=8] {'y','z'}, dimensions={0} | all-to-all | bytes 4980736 | tf_op jit(solution)/shard_map/all_to_all | solution.py:255
  191.0 0.0 reduce-scatter.2.cloned.1.call-done.sum_ref
  191.0 3.1 %finish.1 = (bf16[16,4096]{1,0:T(8,128)(2,1)}, f32[8,16]{1,0:T(8,128)}, bf16[128,1536]{1,0:T(8,128)(2,1)}, f32[256,768]{1,0:T(8,128)}) custom-call(bf16[512,2432]{1,0:T(8,128)(2,1)S(1)} %bitcast.12, bf16[128,1536]{1,0:T(8,128)(2,1)} %bitcast.18, f32[8,16]{1,0:T(8,128)} %bitcast.20, s32[8,16]{1,0:T(8,128)} %bitcast.22, ...), custom_call_target="tpu_custom_call" | custom-call | tf_op jit(solution)/shard_map/finish/pallas_call | solution.py:268
Async XLA Ops:
  7.2 183.9 %reduce-scatter.2.cloned.1.call-start = ((), (), s32[]{:S(2)}) async-start(), calls=%async_computation.3 | async-start | bytes 3538944 | tf_op jit(solution)/shard_map/reduce_scatter | solution.py:267
  104.9 5.3 %collective-permute-start = (bf16[256,2816]{1,0:T(8,128)(2,1)}, bf16[256,2816]{1,0:T(8,128)(2,1)S(1)}, u32[]{:S(2)}, u32[]{:S(2)}) collective-permute-start(bf16[256,2816]{1,0:T(8,128)(2,1)} %get-tuple-element.13), channel_id=1, source_target_pairs={{0,64},{64,0},{1,65},{65,1},{2,66},{66,2},{3,67},{67,3},{4,68},{68... | collective-permute-start | bytes 4325384 | tf_op jit(solution)/shard_map/ppermute | solution.py:254
  110.3 1.1 copy-start
Sparse Core Ops, SparseCore 0:
  117.0 49.0 reduce-scatter.1
